TPU v7x, 32 devices: a whole 2x2x4 slice. The times are simulated.
32 devices in a mesh: lat: 4 (over z), lon: 8 (over y, x, core).
Axes of the slice: x: 2, y: 2, z: 4, core: 2. Of those that a mesh axis runs over, the one named last changes fastest.
Arguments:
- samples: bfloat16 [256, 90112], P(None, ('lat', 'lon')), may hold values from -6 to 6
- area_weight: float32 [90112], P(('lat', 'lon')), may hold values from 0.1 to 1
- ocean_count: int32 [4, 8], P('lat', 'lon'), may hold values from 704 to 2816, as said below
- omega: bfloat16 [512, 256], replicated, may hold values from -5 to 5
Outputs:
- point_basis: bfloat16 [512, 90112], P(None, ('lat', 'lon'))
- sample_basis: float32 [8, 256, 64], replicated
Inputs may be any that keep to these rules, and one draw needn't show every extreme that they name: Each device's block of grid points starts with ocean_count ocean points, the rest are land; some device's block is all ocean (2816).
All inputs are finite; a program needn't handle non-finite values.
Results may differ from a plain program's by a relative error of at most 0.0075.
Values sent between devices are 32-bit elements; how exact they have to be, the bound alone decides.
No kernel may reach another device: no remote copies, remote signals or barrier semaphores. Data moves between devices by JAX's collectives and lax.ppermute only.
A program may use at most 64 MiB of HBM per device.

v0:
```python
import jax
import jax.numpy as jnp
from jax import lax
from jax.sharding import PartitionSpec as P

SAMPLES = 256
COLUMNS = 64
FOLDS = 8


def grid_total(partial_value):
    return lax.psum(partial_value, ("lat", "lon"))


def on_device(samples, area_weight, ocean_count, omega):
    point_cols = samples.shape[1]
    fold_row = lax.iota(jnp.int32, FOLDS * COLUMNS) // COLUMNS
    fold_col = lax.iota(jnp.int32, SAMPLES) // (SAMPLES // FOLDS)
    keeping = fold_row[:, None] != fold_col[None, :]
    live = jnp.where(keeping, omega, jnp.zeros_like(omega))
    valid = lax.iota(jnp.int32, point_cols) < ocean_count[0, 0]
    weighted = jnp.where(
        valid[None, :], samples.astype(jnp.float32) * area_weight[None, :], jnp.float32(0.0)
    ).astype(jnp.bfloat16)
    product = jnp.dot(live, weighted, preferred_element_type=jnp.float32)
    scores = product.astype(jnp.bfloat16)
    folded = scores.reshape(FOLDS, COLUMNS, point_cols)
    devices_all = lax.axis_size("lat") * lax.axis_size("lon")
    total = point_cols * devices_all
    exact = product.reshape(FOLDS, COLUMNS, point_cols)
    partial_gram = jnp.einsum("fkp,fjp->fkj", exact, exact, precision=lax.Precision.HIGHEST)
    gram = grid_total(partial_gram)
    partial_cross = jnp.einsum(
        "sp,fkp->fsk", weighted.astype(jnp.float32), exact, precision=lax.Precision.HIGHEST
    )
    lower_factor = jnp.linalg.cholesky(gram)
    identity = jnp.broadcast_to(jnp.eye(COLUMNS, dtype=jnp.float32), (FOLDS, COLUMNS, COLUMNS))
    inverse = jax.scipy.linalg.solve_triangular(lower_factor, identity, lower=True)
    point_scale = (inverse * jnp.float32(total**0.5)).astype(jnp.bfloat16)
    point_basis = jnp.einsum(
        "fkj,fjp->fkp", point_scale, folded, preferred_element_type=jnp.float32
    )
    point_basis = point_basis.astype(jnp.bfloat16).reshape(FOLDS * COLUMNS, point_cols)
    sample_scale = inverse * jnp.float32((SAMPLES / total) ** 0.5)
    cross = lax.psum(partial_cross, ("lat", "lon"))
    sample_basis = jnp.einsum("fsj,fkj->fsk", cross, sample_scale, precision=lax.Precision.HIGHEST)
    return (point_basis, sample_basis)


def solution(mesh):
    in_specs = (P(None, ("lat", "lon")), P(("lat", "lon")), P("lat", "lon"), P())
    out_specs = (P(None, ("lat", "lon")), P())
    return jax.shard_map(
        on_device, mesh=mesh, in_specs=in_specs, out_specs=out_specs, check_vma=False
    )
```

profile of v0, /device:TPU:0, one launch (start us, length us, event | category | flops | bytes accessed | tf_op | source)
XLA Modules:
  0.0 253.4 jit_solution(10656014839347430208)
XLA Ops:
  7.2 0.0 all-reduce.3.cloned.1.call-start
  7.9 0.0 copy-start
  7.9 0.0 copy-start.1
  7.9 2.5 fusion.26
  10.4 0.0 copy-done
  10.4 0.0 copy-done.1
  10.4 3.7 %fusion.2 = f32[8,256,64]{1,2,0:T(8,128)} fusion(f32[8,64,2816]{2,1,0:T(8,128)S(1)} %bitcast.26, bf16[256,2816]{1,0:T(8,128)(2,1)S(1)} %copy-done, f32[2816]{0:T(1024)S(1)} %copy-done.1, pred[2816]{0:T(1024)(128)(4,1)S(1)} %iota_compare_fusion.2), kind=kOutput, calls=%fused_computation.4 | convolution fusion | flops 4432068608 | bytes 7747328 | tf_op jit(solution)/shard_map/sp,fkp->fsk/dot_general | solution.py:33
  14.1 5.9 %fusion.27 = f32[8,64,64]{1,2,0:T(8,128)} fusion(f32[8,64,2816]{2,1,0:T(8,128)S(1)} %bitcast.27), kind=kOutput, calls=%fused_computation.44 | convolution fusion | flops 1107296256 | bytes 5898240 | tf_op jit(solution)/shard_map/fkp,fjp->fkj/dot_general | solution.py:31
  20.0 0.0 all-reduce.3.cloned.1.call-update
  20.0 132.2 %all-reduce.3.cloned.1.call-done = (f32[8,64,64]{1,2,0:T(8,128)}, f32[8,256,64]{1,2,0:T(8,128)}) async-done(((f32[8,64,64]{1,2,0:T(8,128)}, f32[8,256,64]{1,2,0:T(8,128)}), (f32[8,64,64]{1,2,0:T(8,128)}, f32[8,256,64]{1,2,0:T(8,128)})) %all-reduce.3.cloned.1.call-update) | async-done | bytes 655376 | tf_op jit(solution)/shard_map/psum | solution.py:12
  152.3 1.1 copy.10
  153.4 1.0 fusion.8
  154.3 47.1 %custom-call.8 = f32[8,64,64]{2,1,0:T(8,128)S(1)} custom-call(f32[8,64,64]{2,1,0:T(8,128)S(1)} %fusion.8), custom_call_target="Cholesky" | custom-call | tf_op jit(solution)/shard_map/jit(cholesky)/cholesky | solution.py:36
  201.5 0.1 compare_reduce_fusion
  201.6 0.1 select_bitcast_fusion
  201.7 39.3 %custom-call.9 = f32[8,1,64,64]{2,3,1,0:T(8,128)S(1)} custom-call(f32[8,1,64,64]{3,2,1,0:T(8,128)S(1)} %select_bitcast_fusion), custom_call_target="InvertDiagBlocksLowerTriangular" | custom-call | tf_op jit(solution)/shard_map/jit(_solve_triangular)/vmap()/triangular_solve | solution.py:38
  241.0 0.6 fusion.6
  241.6 2.4 fusion.9
  244.1 2.5 convolution_convert_fusion
  (7 shorter events, 0.1 us)
Async XLA Ops:
  7.2 145.1 %all-reduce.3.cloned.1.call-start = ((), (), s32[]{:S(2)}) async-start(), calls=%async_computation | async-start | bytes 1572864 | tf_op jit(solution)/shard_map/psum | solution.py:12
  7.9 2.5 copy-start
  7.9 2.5 copy-start.1
Sparse Core Ops, SparseCore 0:
  20.1 132.1 all-reduce.2
where the time goes:
time: 254 us; the launch traced here: 253 us
  waiting for transfers between devices  132 us (52%)
  other arithmetic  87.7 us (35%)
  matrix products  17.5 us (7%)
  between operations  14.8 us (6%)
    psum x1, waiting for transfers between devices, grid_total(): return lax.psum(partial_value, ('lat', 'lon'))  132 us
    another operation x4, other arithmetic, on_device(): lower_factor = jnp.linalg.cholesky(gram)  47.2 us
    another operation x3, other arithmetic, on_device(): jax.scipy.linalg.solve_triangular(lower_factor, identity, lower=True)  39.4 us
    dot_general x1, matrix products, on_device(): jnp.einsum('fkp,fjp->fkj', exact, exact, precision=lax.Precision.HIGHEST)  5.85 us
  transfers between devices with their start and end apart: 1, of which 1 were waited for; matrix products, arithmetic and copies ran while one was open for 0% of the time, Pallas kernels for 0%

commit v1 on v0

--- a/solution.py
+++ b/solution.py
@@ -9,7 +9,7 @@
 
 
 def grid_total(partial_value):
-    return lax.psum(partial_value, ("lat", "lon"))
+    return jnp.sum(lax.all_gather(partial_value, ("lat", "lon")), axis=0)
 
 
 def on_device(samples, area_weight, ocean_count, omega):

time: 254 us -> 243 us (0.957)
  waiting for transfers between devices: 132 us -> 110 us
  other arithmetic: 87.7 us -> 93 us
  matrix products: 17.5 us -> 21.7 us
    psum x1, waiting for transfers between devices: 132 us -> 36.5 us  [on_device(): cross = lax.psum(partial_cross, ('lat', 'lon'))]
    all_gather x0 -> x1, waiting for transfers between devices: none -> 73.3 us  [grid_total(): return jnp.sum(lax.all_gather(partial_value, ('lat', 'lon')), axis=0)]
    reduce_sum x0 -> x1, other arithmetic: none -> 4.41 us  [grid_total(): return jnp.sum(lax.all_gather(partial_value, ('lat', 'lon')), axis=0)]
    dot_general x1, matrix products: 3.7 us -> 6.7 us  [on_device(): jnp.einsum('sp,fkp->fsk', weighted.astype(jnp.float32), exact, precision=...]
  transfers between devices with their start and end apart: 1 -> 2, of which waited for: 1 -> 2; matrix products, arithmetic and copies ran while one was open for 0% -> 43% of each run, Pallas kernels for 0% -> 0%
where the time goes in v1:
time: 243 us; the launch traced here: 242 us
  waiting for transfers between devices  110 us (45%)
  other arithmetic  93 us (38%)
  matrix products  21.7 us (9%)
  between operations  14.8 us (6%)
  local copies, waits for them, and re-layouts  2.67 us (1%)
    all_gather x1, waiting for transfers between devices, grid_total(): return jnp.sum(lax.all_gather(partial_value, ('lat', 'lon')), axis=0)  73.3 us
    another operation x4, other arithmetic, on_device(): lower_factor = jnp.linalg.cholesky(gram)  47.8 us
    another operation x3, other arithmetic, on_device(): jax.scipy.linalg.solve_triangular(lower_factor, identity, lower=True)  40.1 us
    psum x1, waiting for transfers between devices, on_device(): cross = lax.psum(partial_cross, ('lat', 'lon'))  36.5 us
    dot_general x1, matrix products, on_device(): jnp.einsum('sp,fkp->fsk', weighted.astype(jnp.float32), exact, precision=...  6.7 us
    dot_general x1, matrix products, on_device(): jnp.einsum('fkp,fjp->fkj', exact, exact, precision=lax.Precision.HIGHEST)  6.2 us
  transfers between devices with their start and end apart: 2, of which 2 were waited for; matrix products, arithmetic and copies ran while one was open for 43% of the time, Pallas kernels for 0%

profile of v1, /device:TPU:0, one launch (start us, length us, event | category | flops | bytes accessed | tf_op | source)
XLA Modules:
  0.0 242.2 jit_solution(11312542352633324221)
XLA Ops:
  7.2 0.0 all-gather.3.cloned.1.call-start
  7.9 2.4 fusion.26
  10.3 0.0 copy-start
  10.3 2.5 %copy-done = f32[512,2816]{1,0:T(8,128)} copy-done((f32[512,2816]{1,0:T(8,128)}, f32[512,2816]{1,0:T(8,128)S(1)}, u32[]{:S(2)}) %copy-start) | copy-done | bytes 5767192
  12.8 0.0 copy-start.1
  12.8 6.2 %fusion.27 = f32[8,64,64]{2,1,0:T(8,128)} fusion(f32[8,64,2816]{2,1,0:T(8,128)S(1)} %bitcast.27), kind=kOutput, calls=%fused_computation.44 | convolution fusion | flops 1107296256 | bytes 5898240 | tf_op jit(solution)/shard_map/fkp,fjp->fkj/dot_general | solution.py:31
  19.0 0.0 all-gather.3.cloned.1.call-update
  19.0 0.2 all-reduce.2.cloned.1.call-start
  19.3 0.0 copy-done.1
  19.3 6.7 %fusion.2 = f32[8,256,64]{1,2,0:T(8,128)} fusion(f32[8,64,2816]{2,1,0:T(8,128)} %bitcast.28, bf16[256,2816]{1,0:T(8,128)(2,1)} %param.4, f32[2816]{0:T(1024)S(1)} %copy-done.1, pred[2816]{0:T(1024)(128)(4,1)S(1)} %iota_compare_fusion.2), kind=kOutput, calls=%fused_computation.4 | convolution fusion | flops 4432068608 | bytes 7747328 | tf_op jit(solution)/shard_map/sp,fkp->fsk/dot_general | solution.py:33
  26.0 0.0 all-reduce.2.cloned.1.call-update
  26.0 73.3 %all-gather.3.cloned.1.call-done = f32[256,64,64]{2,1,0:T(8,128)} async-done(((f32[8,64,64]{2,1,0:T(8,128)}), f32[256,64,64]{2,1,0:T(8,128)}) %all-gather.3.cloned.1.call-update) | async-done | bytes 4194320 | tf_op jit(solution)/shard_map/all_gather | solution.py:12
  99.3 4.4 %reduce_sum.9 = f32[8,64,64]{2,1,0:T(8,128)S(1)} reduce(f32[32,8,64,64]{3,2,1,0:T(8,128)} %bitcast.30, f32[]{:T(128)} %constant.79.clone.1), dimensions={0}, to_apply=%region_0.1 | reduce | flops 1015808 | bytes 4325380 | tf_op jit(solution)/shard_map/reduce_sum | solution.py:12
  103.7 0.1 copy.10
  103.9 0.7 fusion.8
  104.6 47.6 %custom-call.8 = f32[8,64,64]{2,1,0:T(8,128)S(1)} custom-call(f32[8,64,64]{2,1,0:T(8,128)} %fusion.8), custom_call_target="Cholesky" | custom-call | tf_op jit(solution)/shard_map/jit(cholesky)/cholesky | solution.py:36
  152.3 0.1 compare_reduce_fusion
  152.4 0.1 select_bitcast_fusion
  152.5 40.0 %custom-call.9 = f32[8,1,64,64]{2,3,1,0:T(8,128)} custom-call(f32[8,1,64,64]{3,2,1,0:T(8,128)S(1)} %select_bitcast_fusion), custom_call_target="InvertDiagBlocksLowerTriangular" | custom-call | tf_op jit(solution)/shard_map/jit(_solve_triangular)/vmap()/triangular_solve | solution.py:38
  192.5 1.5 fusion.6
  194.0 2.5 %convolution_convert_fusion = bf16[8,64,2816]{2,1,0:T(8,128)(2,1)} fusion(bf16[8,64,2816]{2,1,0:T(8,128)(2,1)S(1)} %bitcast.29, f32[8,64,64]{2,1,0:T(8,128)S(1)} %fusion.6), kind=kOutput, calls=%fused_computation | convolution fusion | flops 186056704 | bytes 5898240 | tf_op jit(solution)/shard_map/fkj,fjp->fkp/dot_general | solution.py:40
  196.5 36.5 %all-reduce.2.cloned.1.call-done = f32[8,256,64]{1,2,0:T(8,128)} async-done(((f32[8,256,64]{1,2,0:T(8,128)}), f32[8,256,64]{1,2,0:T(8,128)}) %all-reduce.2.cloned.1.call-update) | async-done | bytes 524304 | tf_op jit(solution)/shard_map/psum | solution.py:45
  233.0 2.4 %fusion.9 = f32[8,256,64]{1,2,0:T(8,128)} fusion(f32[8,256,64]{1,2,0:T(8,128)} %all-reduce.2.cloned.1.call-done, f32[8,64,64]{2,1,0:T(8,128)S(1)} %fusion.6), kind=kOutput, calls=%fused_computation.11 | convolution fusion | flops 100696064 | bytes 1179648 | tf_op jit(solution)/shard_map/fsj,fkj->fsk/dot_general | solution.py:46
  (7 shorter events, 0.1 us)
Async XLA Ops:
  7.2 92.1 %all-gather.3.cloned.1.call-start = ((), (), s32[]{:S(2)}) async-start(), calls=%async_computation.1 | async-start | bytes 8650752 | tf_op jit(solution)/shard_map/all_gather | solution.py:12
  10.3 2.5 %copy-start = (f32[512,2816]{1,0:T(8,128)}, f32[512,2816]{1,0:T(8,128)S(1)}, u32[]{:S(2)}) copy-start(f32[512,2816]{1,0:T(8,128)S(1)} %get-tuple-element.3) | copy-start | bytes 17301508
  12.8 6.5 %copy-start.1 = (f32[2816]{0:T(1024)S(1)}, f32[2816]{0:T(1024)}, u32[]{:S(2)}) copy-start(f32[2816]{0:T(1024)} %param.5) | copy-start | bytes 33796
  19.0 213.9 %all-reduce.2.cloned.1.call-start = ((), (), s32[]{:S(2)}) async-start(), calls=%async_computation | async-start | bytes 1048576 | tf_op jit(solution)/shard_map/psum | solution.py:45
Sparse Core Ops, SparseCore 0:
  19.2 80.1 all-gather.2
  105.2 127.7 all-reduce.1
